TPU v7x, 32 devices: a whole 2x2x4 slice. The times are simulated.
32 devices in a mesh: mom: 4 (over y, x), sec: 8 (over z, core).
Axes of the slice: x: 2, y: 2, z: 4, core: 2. Of those that a mesh axis runs over, the one named last changes fastest.
Arguments:
- left_env: bfloat16 [64, 64, 2816], P('sec', 'mom'), may hold values from -0.75 to 0.75
- right_env: bfloat16 [64, 64, 2816], P('sec', 'mom'), may hold values from -0.109375 to 0.109375
- left_mixed: bfloat16 [4, 64, 64, 2816], P('mom', 'sec'), may hold values from -0.75 to 0.75
- excitation: bfloat16 [4, 64, 64, 256], P('mom', 'sec'), may hold values from -6 to 6
- ground: bfloat16 [64, 64, 256], P('sec'), may hold values from -6 to 6
- mpo: bfloat16 [44, 4, 44, 4], replicated, may hold values from -0.4375 to 0.4375
- momentum: int32 [4], P('mom'), may hold values from 0 to 3, each once
- block_dims: int32 [64], P('sec'), may hold values from 16 to 64, as said below
Outputs:
- excited: bfloat16 [4, 2, 64, 64, 256], P('mom', None, 'sec')
Inputs may be any that keep to these rules, and one draw needn't show every extreme that they name: `block_dims`: every block has at least 16 used rows; some block uses all 64 and some exactly 16.
All inputs are finite; a program needn't handle non-finite values.
Results may differ from a plain program's by a relative error of at most 0.0058.
Values may be sent and summed in bfloat16 or wider, within the bound.
No kernel may reach another device: no remote copies, remote signals or barrier semaphores. Data moves between devices by JAX's collectives and lax.ppermute only.
A program may use at most 128 MiB of HBM per device.

v0:
```python
import math
import jax
import jax.numpy as jnp
from jax import lax
from jax.sharding import PartitionSpec as P


def with_halo(shard, sides, width):
    for axis, dim in sides:
        devices, length = (lax.axis_size(axis), shard.shape[dim])
        up = [(i, (i + 1) % devices) for i in range(devices - 1)]
        down = [(j, i) for i, j in up]
        last = lax.slice_in_dim(shard, length - width, length, axis=dim)
        initial = lax.slice_in_dim(shard, 0, width, axis=dim)
        before = lax.ppermute(last, axis, up)
        after = lax.ppermute(initial, axis, down)
        shard = jnp.concatenate([before, shard, after], axis=dim)
    return shard


def apply_term(left, source, right, mpo):
    width = left.shape[1]
    low = width // 3
    high = width - low
    bounds = [(0, low), (low, high), (high, width)]
    count = source.shape[0]
    rows = left.shape[0]
    block = right.shape[0]
    wide = source.shape[-1]
    phys = wide // block
    total = None
    for shift in range(3):
        start, stop = bounds[shift]
        temp = jnp.einsum(
            "iwa,nab->niwb",
            left[:, start:stop, :],
            source[:, shift],
            preferred_element_type=jnp.float32,
        ).astype(jnp.bfloat16)
        temp = temp.reshape(count, rows, stop - start, phys, block)
        part_sum = jnp.einsum(
            "niwpj,wpvq->nviqj", temp, mpo[start:stop], preferred_element_type=jnp.float32
        )
        total = part_sum if total is None else total + part_sum
    mixed = total.astype(jnp.bfloat16)
    result = jnp.einsum("nviqj,jvk->niqk", mixed, right, preferred_element_type=jnp.float32)
    return result.reshape(count, rows, wide)


def shards(left_env, right_env, left_mixed, excitation, ground, mpo, momentum, block_dims):
    sectors = excitation.shape[1]
    block = excitation.shape[2]
    wide = excitation.shape[3]
    width = left_env.shape[2] // block
    groups = lax.axis_size("mom")
    right_full = lax.all_gather(right_env, "mom", axis=1, tiled=True)
    stacked = jnp.stack([excitation[0], ground])
    padded = with_halo(stacked, (("sec", 1),), 1)
    sector_ids = jnp.arange(sectors, dtype=jnp.int32)

    def shifted_sector(sector):
        right = right_full[sector].reshape(block, width, block)
        mixl = left_mixed[0, sector].reshape(block, width, block)
        src = lax.dynamic_slice_in_dim(padded[1:2], sector, 3, 1)
        return apply_term(mixl, src, right, mpo)[0]

    shifted = lax.map(shifted_sector, sector_ids)
    left_full = lax.all_gather(left_env, "mom", axis=1, tiled=True)

    def direct_sector(sector):
        right = right_full[sector].reshape(block, width, block)
        left = left_full[sector].reshape(block, width, block)
        src = lax.dynamic_slice_in_dim(padded[0:1], sector, 3, 1)
        return apply_term(left, src, right, mpo)[0]

    direct = lax.map(direct_sector, sector_ids)
    phase = 2.0 * math.pi * momentum[0].astype(jnp.float32) / groups
    rows_idx = jnp.arange(block, dtype=jnp.int32)
    cols_idx = jnp.arange(wide, dtype=jnp.int32) % block
    used = block_dims[:, None, None]
    mask = ((rows_idx[None, :, None] < used) & (cols_idx[None, None, :] < used)).astype(jnp.float32)
    real_part = mask * (direct + jnp.cos(phase) * shifted)
    imag_part = -mask * jnp.sin(phase) * shifted
    return jnp.stack([real_part, imag_part])[None].astype(jnp.bfloat16)


def solution(mesh):
    return jax.shard_map(
        shards,
        mesh=mesh,
        in_specs=(
            P("sec", "mom", None),
            P("sec", "mom", None),
            P("mom", "sec", None, None),
            P("mom", "sec", None, None),
            P("sec", None, None),
            P(),
            P("mom"),
            P("sec"),
        ),
        out_specs=P("mom", None, "sec", None, None),
        check_vma=False,
    )
```

profile of v0, /device:TPU:0, one launch (start us, length us, event | category | flops | bytes accessed | tf_op | source)
XLA Modules:
  0.0 640.0 jit_solution(17581412542030367887)
XLA Ops:
  18.7 35.0 %all-gather.3.cloned.1.call-done = bf16[8,64,2816]{2,1,0:T(8,128)(2,1)} async-done(((bf16[8,16,2816]{2,1,0:T(8,128)(2,1)}), bf16[8,64,2816]{2,1,0:T(8,128)(2,1)}) %all-gather.3.cloned.1.call-update) | async-done | bytes 2883600 | tf_op jit(solution)/shard_map/all_gather | solution.py:68
  53.7 43.7 %all-gather.5.cloned.1.call-done = bf16[8,64,2816]{2,1,0:T(8,128)(2,1)} async-done(((bf16[8,16,2816]{2,1,0:T(8,128)(2,1)}), bf16[8,64,2816]{2,1,0:T(8,128)(2,1)}) %all-gather.5.cloned.1.call-update) | async-done | bytes 2883600 | tf_op jit(solution)/shard_map/all_gather | solution.py:56
  98.3 268.4 %while.20 = (s32[]{:T(128)}, f32[8,64,256]{2,1,0:T(8,128)}, bf16[2,10,64,256]{3,2,1,0:T(8,128)(2,1)S(1)}, s32[8]{0:T(128)S(1)}, bf16[8,64,2816]{2,1,0:T(8,128)(2...) while((s32[]{:T(128)}, f32[8,64,256]{2,1,0:T(8,128)}, ...), condition=%wide.region_1.2_spmd, body=%wide.region_0.1_spmd.sunk | while | flops 441188352 | bytes 44241284 | solution.py:76
  115.9 6.3 fusion.110
  122.3 5.2 copy.125
  149.5 6.3 fusion.110
  155.8 5.2 copy.125
  183.0 6.3 fusion.110
  216.6 6.3 fusion.110
  222.9 5.2 copy.125
  250.1 6.3 fusion.110
  256.5 5.2 copy.125
  283.7 6.3 fusion.110
  317.3 6.3 fusion.110
  350.8 6.3 fusion.110
  367.5 263.4 %while.21 = (s32[]{:T(128)}, f32[8,64,256]{2,1,0:T(8,128)}, bf16[2,10,64,256]{3,2,1,0:T(8,128)(2,1)S(1)}, s32[8]{0:T(128)S(1)}, bf16[1,8,64,2816]{3,2,1,0:T(8,12...) while((s32[]{:T(128)}, f32[8,64,256]{2,1,0:T(8,128)}, ...), condition=%wide.region_3.4_spmd, body=%wide.region_2.3_spmd.sunk | while | flops 441188352 | bytes 43225452 | solution.py:67
  383.5 6.3 fusion.128
  416.4 6.3 fusion.128
  449.3 6.3 fusion.128
  482.3 6.3 fusion.128
  515.2 6.3 fusion.128
  548.1 6.3 fusion.128
  581.1 6.3 fusion.128
  614.0 6.3 fusion.128
  (492 shorter events, 372.1 us)
Async XLA Ops:
  6.5 47.2 %all-gather.3.cloned.1.call-start = ((), (), s32[]{:S(2)}) async-start(), calls=%async_computation | async-start | bytes 3604480 | tf_op jit(solution)/shard_map/all_gather | solution.py:68
  7.3 90.2 %all-gather.5.cloned.1.call-start = ((), (), s32[]{:S(2)}) async-start(), calls=%async_computation.1 | async-start | bytes 3604480 | tf_op jit(solution)/shard_map/all_gather | solution.py:56
  8.8 8.7 %collective-permute-start.1 = (bf16[2,1,64,256]{3,2,1,0:T(8,128)(2,1)S(1)}, bf16[2,1,64,256]{3,2,1,0:T(8,128)(2,1)S(1)}, u32[]{:S(2)}, u32[]{:S(2)}) collective-permute-start(bf16[2,1,64,256]{3,2,1,0:T(8,128)(2,1)S(1)} %get-tuple-element.146), channel_id=1, source_target_pairs={{1,0},{2,1},{3,2},{4,3},{5,4},{6,5},{7,6},{9,8},{10,9},{11,10},{12... | collective-permute-start | bytes 196616 | tf_op jit(solution)/shard_map/ppermute | solution.py:16
  10.1 7.4 %collective-permute-start = (bf16[2,1,64,256]{3,2,1,0:T(8,128)(2,1)S(1)}, bf16[2,1,64,256]{3,2,1,0:T(8,128)(2,1)S(1)}, u32[]{:S(2)}, u32[]{:S(2)}) collective-permute-start(bf16[2,1,64,256]{3,2,1,0:T(8,128)(2,1)S(1)} %get-tuple-element.145), channel_id=1, source_target_pairs={{0,1},{1,2},{2,3},{3,4},{4,5},{5,6},{6,7},{8,9},{9,10},{10,11},{11... | collective-permute-start | bytes 196616 | tf_op jit(solution)/shard_map/ppermute | solution.py:15
  98.3 11.6 %copy-start = (bf16[44,4,44,4]{2,0,1,3:T(8,128)(2,1)}, bf16[44,4,44,4]{2,0,1,3:T(8,128)(2,1)S(1)}, u32[]{:S(2)}) copy-start(bf16[44,4,44,4]{2,0,1,3:T(8,128)(2,1)S(1)} %get-tuple-element.276) | copy-start | bytes 185860 | tf_op jit(solution)/shard_map/while
  131.8 5.7 copy-start.4
  131.8 11.6 %copy-start = (bf16[44,4,44,4]{2,0,1,3:T(8,128)(2,1)}, bf16[44,4,44,4]{2,0,1,3:T(8,128)(2,1)S(1)}, u32[]{:S(2)}) copy-start(bf16[44,4,44,4]{2,0,1,3:T(8,128)(2,1)S(1)} %get-tuple-element.276) | copy-start | bytes 185860 | tf_op jit(solution)/shard_map/while
  165.4 5.7 copy-start.4
  165.4 11.6 %copy-start = (bf16[44,4,44,4]{2,0,1,3:T(8,128)(2,1)}, bf16[44,4,44,4]{2,0,1,3:T(8,128)(2,1)S(1)}, u32[]{:S(2)}) copy-start(bf16[44,4,44,4]{2,0,1,3:T(8,128)(2,1)S(1)} %get-tuple-element.276) | copy-start | bytes 185860 | tf_op jit(solution)/shard_map/while
  198.9 11.6 %copy-start = (bf16[44,4,44,4]{2,0,1,3:T(8,128)(2,1)}, bf16[44,4,44,4]{2,0,1,3:T(8,128)(2,1)S(1)}, u32[]{:S(2)}) copy-start(bf16[44,4,44,4]{2,0,1,3:T(8,128)(2,1)S(1)} %get-tuple-element.276) | copy-start | bytes 185860 | tf_op jit(solution)/shard_map/while
  232.5 11.6 %copy-start = (bf16[44,4,44,4]{2,0,1,3:T(8,128)(2,1)}, bf16[44,4,44,4]{2,0,1,3:T(8,128)(2,1)S(1)}, u32[]{:S(2)}) copy-start(bf16[44,4,44,4]{2,0,1,3:T(8,128)(2,1)S(1)} %get-tuple-element.276) | copy-start | bytes 185860 | tf_op jit(solution)/shard_map/while
  266.0 11.6 %copy-start = (bf16[44,4,44,4]{2,0,1,3:T(8,128)(2,1)}, bf16[44,4,44,4]{2,0,1,3:T(8,128)(2,1)S(1)}, u32[]{:S(2)}) copy-start(bf16[44,4,44,4]{2,0,1,3:T(8,128)(2,1)S(1)} %get-tuple-element.276) | copy-start | bytes 185860 | tf_op jit(solution)/shard_map/while
  299.6 11.6 %copy-start = (bf16[44,4,44,4]{2,0,1,3:T(8,128)(2,1)}, bf16[44,4,44,4]{2,0,1,3:T(8,128)(2,1)S(1)}, u32[]{:S(2)}) copy-start(bf16[44,4,44,4]{2,0,1,3:T(8,128)(2,1)S(1)} %get-tuple-element.276) | copy-start | bytes 185860 | tf_op jit(solution)/shard_map/while
  333.2 11.6 %copy-start = (bf16[44,4,44,4]{2,0,1,3:T(8,128)(2,1)}, bf16[44,4,44,4]{2,0,1,3:T(8,128)(2,1)S(1)}, u32[]{:S(2)}) copy-start(bf16[44,4,44,4]{2,0,1,3:T(8,128)(2,1)S(1)} %get-tuple-element.276) | copy-start | bytes 185860 | tf_op jit(solution)/shard_map/while
  367.5 263.4 %copy-start.9 = (pred[8,256]{1,0:T(8,128)(4,1)S(1)}, pred[8,256]{1,0:T(8,128)(4,1)}, u32[]{:S(2)}) copy-start(pred[8,256]{1,0:T(8,128)(4,1)} %broadcast_compare_fusion) | copy-start | bytes 6148
  367.5 263.4 %copy-start.10 = (pred[8,64]{1,0:T(8,128)(4,1)S(1)}, pred[8,64]{1,0:T(8,128)(4,1)}, u32[]{:S(2)}) copy-start(pred[8,64]{1,0:T(8,128)(4,1)} %iota_compare_fusion) | copy-start | bytes 1540
  367.5 10.7 %copy-start.2 = (bf16[44,4,44,4]{2,0,1,3:T(8,128)(2,1)}, bf16[44,4,44,4]{2,0,1,3:T(8,128)(2,1)S(1)}, u32[]{:S(2)}) copy-start(bf16[44,4,44,4]{2,0,1,3:T(8,128)(2,1)S(1)} %get-tuple-element.315) | copy-start | bytes 185860 | tf_op jit(solution)/shard_map/while
  400.4 10.8 %copy-start.2 = (bf16[44,4,44,4]{2,0,1,3:T(8,128)(2,1)}, bf16[44,4,44,4]{2,0,1,3:T(8,128)(2,1)S(1)}, u32[]{:S(2)}) copy-start(bf16[44,4,44,4]{2,0,1,3:T(8,128)(2,1)S(1)} %get-tuple-element.315) | copy-start | bytes 185860 | tf_op jit(solution)/shard_map/while
  433.3 10.8 %copy-start.2 = (bf16[44,4,44,4]{2,0,1,3:T(8,128)(2,1)}, bf16[44,4,44,4]{2,0,1,3:T(8,128)(2,1)S(1)}, u32[]{:S(2)}) copy-start(bf16[44,4,44,4]{2,0,1,3:T(8,128)(2,1)S(1)} %get-tuple-element.315) | copy-start | bytes 185860 | tf_op jit(solution)/shard_map/while
  466.2 10.8 %copy-start.2 = (bf16[44,4,44,4]{2,0,1,3:T(8,128)(2,1)}, bf16[44,4,44,4]{2,0,1,3:T(8,128)(2,1)S(1)}, u32[]{:S(2)}) copy-start(bf16[44,4,44,4]{2,0,1,3:T(8,128)(2,1)S(1)} %get-tuple-element.315) | copy-start | bytes 185860 | tf_op jit(solution)/shard_map/while
  499.2 10.8 %copy-start.2 = (bf16[44,4,44,4]{2,0,1,3:T(8,128)(2,1)}, bf16[44,4,44,4]{2,0,1,3:T(8,128)(2,1)S(1)}, u32[]{:S(2)}) copy-start(bf16[44,4,44,4]{2,0,1,3:T(8,128)(2,1)S(1)} %get-tuple-element.315) | copy-start | bytes 185860 | tf_op jit(solution)/shard_map/while
  532.1 10.8 %copy-start.2 = (bf16[44,4,44,4]{2,0,1,3:T(8,128)(2,1)}, bf16[44,4,44,4]{2,0,1,3:T(8,128)(2,1)S(1)}, u32[]{:S(2)}) copy-start(bf16[44,4,44,4]{2,0,1,3:T(8,128)(2,1)S(1)} %get-tuple-element.315) | copy-start | bytes 185860 | tf_op jit(solution)/shard_map/while
  565.0 10.8 %copy-start.2 = (bf16[44,4,44,4]{2,0,1,3:T(8,128)(2,1)}, bf16[44,4,44,4]{2,0,1,3:T(8,128)(2,1)S(1)}, u32[]{:S(2)}) copy-start(bf16[44,4,44,4]{2,0,1,3:T(8,128)(2,1)S(1)} %get-tuple-element.315) | copy-start | bytes 185860 | tf_op jit(solution)/shard_map/while
  598.0 10.8 %copy-start.2 = (bf16[44,4,44,4]{2,0,1,3:T(8,128)(2,1)}, bf16[44,4,44,4]{2,0,1,3:T(8,128)(2,1)S(1)}, u32[]{:S(2)}) copy-start(bf16[44,4,44,4]{2,0,1,3:T(8,128)(2,1)S(1)} %get-tuple-element.315) | copy-start | bytes 185860 | tf_op jit(solution)/shard_map/while
  (54 other events, 232.5 us)
Sparse Core Ops, SparseCore 0:
  9.2 44.4 all-gather.2
  55.6 41.7 all-gather.4
where the time goes:
time: 643 us; the launch traced here: 640 us
  matrix products  291 us (45%)
  local copies, waits for them, and re-layouts  191 us (30%)
  waiting for transfers between devices  80.1 us (12%)
  loops' own time  52.6 us (8%)
  between operations  14.3 us (2%)
  other arithmetic  6.82 us (1%)
    dot_general x48, matrix products, apply_term(): jnp.einsum('niwpj,wpvq->nviqj', temp, mpo[start:stop], preferred_element_...  220 us
    another operation x66, local copies, waits for them, and re-layouts  119 us
    dot_general x16, matrix products, apply_term(): jnp.einsum('nviqj,jvk->niqk', mixed, right, preferred_element_type=jnp.fl...  46.1 us
    all_gather x1, waiting for transfers between devices, shards(): right_full = lax.all_gather(right_env, 'mom', axis=1, tiled=True)  43.7 us
    all_gather x1, waiting for transfers between devices, shards(): left_full = lax.all_gather(left_env, 'mom', axis=1, tiled=True)  35 us
    another operation x1, loops' own time, shards(): shifted = lax.map(shifted_sector, sector_ids)  26.6 us
    another operation x1, loops' own time, shards(): direct = lax.map(direct_sector, sector_ids)  26 us
    dot_general x48, matrix products, apply_term(): jnp.einsum('iwa,nab->niwb', left[:, start:stop, :], source[:, shift], pre...  25 us
  transfers between devices with their start and end apart: 4, of which 2 were waited for; matrix products, arithmetic and copies ran while one was open for 1% of the time, Pallas kernels for 0%

commit v1 on v0

--- a/solution.py
+++ b/solution.py
@@ -53,7 +53,15 @@
     wide = excitation.shape[3]
     width = left_env.shape[2] // block
     groups = lax.axis_size("mom")
-    right_full = lax.all_gather(right_env, "mom", axis=1, tiled=True)
+    ways, here = (lax.axis_size("mom"), lax.axis_index("mom"))
+    grown, reach = (right_env, 1)
+    while reach < ways:
+        theirs = lax.ppermute(grown, "mom", [(d, d ^ reach) for d in range(ways)])
+        mine_first = jnp.concatenate([grown, theirs], axis=1)
+        theirs_first = jnp.concatenate([theirs, grown], axis=1)
+        grown = jnp.where(here & reach == 0, mine_first, theirs_first)
+        reach = 2 * reach
+    right_full = grown
     stacked = jnp.stack([excitation[0], ground])
     padded = with_halo(stacked, (("sec", 1),), 1)
     sector_ids = jnp.arange(sectors, dtype=jnp.int32)

time: 643 us -> 621 us (0.966)
  waiting for transfers between devices: 80.1 us -> 47.7 us
    ppermute x0 -> x2, waiting for transfers between devices: none -> 47.7 us  [shards(): theirs = lax.ppermute(grown, 'mom', [(d, d ^ reach) for d in range(ways)])]
    all_gather x1 -> x0, waiting for transfers between devices: 43.7 us -> none  [shards(): right_full = lax.all_gather(right_env, 'mom', axis=1, tiled=True)]
    all_gather x1, waiting for transfers between devices: 35 us -> 0.01 us  [shards(): left_full = lax.all_gather(left_env, 'mom', axis=1, tiled=True)]
    dot_general x48, matrix products: 220 us -> 233 us  [apply_term(): jnp.einsum('niwpj,wpvq->nviqj', temp, mpo[start:stop], preferred_element_...]
    dot_general x48, matrix products: 25 us -> 12.9 us  [apply_term(): jnp.einsum('iwa,nab->niwb', left[:, start:stop, :], source[:, shift], pre...]
  transfers between devices with their start and end apart: 4 -> 5, of which waited for: 2 -> 2; matrix products, arithmetic and copies ran while one was open for 1% -> 39% of each run, Pallas kernels for 0% -> 0%
where the time goes in v1:
time: 621 us; the launch traced here: 618 us
  matrix products  293 us (47%)
  local copies, waits for them, and re-layouts  191 us (31%)
  loops' own time  54.3 us (9%)
  waiting for transfers between devices  47.7 us (8%)
  between operations  14.3 us (2%)
  other arithmetic  9.74 us (2%)
  starting transfers between devices  9.2 us (1%)
    dot_general x48, matrix products, apply_term(): jnp.einsum('niwpj,wpvq->nviqj', temp, mpo[start:stop], preferred_element_...  233 us
    another operation x66, local copies, waits for them, and re-layouts  119 us
    ppermute x2, waiting for transfers between devices, shards(): theirs = lax.ppermute(grown, 'mom', [(d, d ^ reach) for d in range(ways)])  47.7 us
    dot_general x16, matrix products, apply_term(): jnp.einsum('nviqj,jvk->niqk', mixed, right, preferred_element_type=jnp.fl...  46.4 us
    another operation x1, loops' own time, shards(): shifted = lax.map(shifted_sector, sector_ids)  27.9 us
    another operation x1, loops' own time, shards(): direct = lax.map(direct_sector, sector_ids)  26.5 us
    dot_general x48, matrix products, apply_term(): jnp.einsum('iwa,nab->niwb', left[:, start:stop, :], source[:, shift], pre...  12.9 us
  transfers between devices with their start and end apart: 5, of which 2 were waited for; matrix products, arithmetic and copies ran while one was open for 39% of the time, Pallas kernels for 0%

profile of v1, /device:TPU:0, one launch (start us, length us, event | category | flops | bytes accessed | tf_op | source)
XLA Modules:
  0.0 618.5 jit_solution(10491832465465088563)
XLA Ops:
  9.6 16.3 %collective-permute-done.2 = bf16[8,16,2816]{2,1,0:T(8,128)(2,1)S(1)} collective-permute-done((bf16[8,16,2816]{2,1,0:T(8,128)(2,1)}, bf16[8,16,2816]{2,1,0:T(8,128)(2,1)S(1)}, u32[]{:S(2)}, u32[]{:S(2)}) %collective-permute-start.2) | collective-permute-done | bytes 720928 | tf_op jit(solution)/shard_map/ppermute | solution.py:59
  36.9 31.3 %collective-permute-done.3 = bf16[8,32,2816]{2,1,0:T(8,128)(2,1)} collective-permute-done((bf16[8,32,2816]{2,1,0:T(8,128)(2,1)S(1)}, bf16[8,32,2816]{2,1,0:T(8,128)(2,1)}, u32[]{:S(2)}, u32[]{:S(2)}) %collective-permute-start.3) | collective-permute-done | bytes 1441824 | tf_op jit(solution)/shard_map/ppermute | solution.py:59
  72.7 264.8 %while.21 = (s32[]{:T(128)}, f32[8,64,256]{2,1,0:T(8,128)}, bf16[2,10,64,256]{3,2,1,0:T(8,128)(2,1)S(1)}, s32[8]{0:T(128)S(1)}, bf16[1,8,64,2816]{3,2,1,0:T(8,12...) while((s32[]{:T(128)}, f32[8,64,256]{2,1,0:T(8,128)}, ...), condition=%wide.region_3.4_spmd, body=%wide.region_2.3_spmd.sunk | while | flops 441188352 | bytes 35455284 | solution.py:75
  89.0 6.3 %fusion.128 = bf16[44,64,4,64]{3,0,2,1:T(8,128)(2,1)S(1)} fusion(f32[64,64,44,4,1]{1,2,4,3,0:T(8,128)} %fusion.123, f32[64,64,44,4,1]{1,2,4,3,0:T(8,128)} %fusion.126, bf16[64,14,4,64,1]{3,2,0,1,4:T(4,128)(2,1)} %bitcast.261, bf16[44,4,44,4]{2,0,1,3:T(8,128)(2,1)S(1)} %get-tuple-element.315), kind=kOutput, calls=%fused_computation.38.clone.1 | convolution fusion | flops 82903040 | bytes 7733248 | tf_op jit(solution)/shard_map/while/body/eval_jaxpr/niwpj,wpvq->nviqj/dot_general | solution.py:41
  95.3 5.2 copy.133
  122.1 6.3 %fusion.128 = bf16[44,64,4,64]{3,0,2,1:T(8,128)(2,1)S(1)} fusion(f32[64,64,44,4,1]{1,2,4,3,0:T(8,128)} %fusion.123, f32[64,64,44,4,1]{1,2,4,3,0:T(8,128)} %fusion.126, bf16[64,14,4,64,1]{3,2,0,1,4:T(4,128)(2,1)} %bitcast.261, bf16[44,4,44,4]{2,0,1,3:T(8,128)(2,1)S(1)} %get-tuple-element.315), kind=kOutput, calls=%fused_computation.38.clone.1 | convolution fusion | flops 82903040 | bytes 7733248 | tf_op jit(solution)/shard_map/while/body/eval_jaxpr/niwpj,wpvq->nviqj/dot_general | solution.py:41
  128.4 5.2 copy.133
  155.2 6.3 %fusion.128 = bf16[44,64,4,64]{3,0,2,1:T(8,128)(2,1)S(1)} fusion(f32[64,64,44,4,1]{1,2,4,3,0:T(8,128)} %fusion.123, f32[64,64,44,4,1]{1,2,4,3,0:T(8,128)} %fusion.126, bf16[64,14,4,64,1]{3,2,0,1,4:T(4,128)(2,1)} %bitcast.261, bf16[44,4,44,4]{2,0,1,3:T(8,128)(2,1)S(1)} %get-tuple-element.315), kind=kOutput, calls=%fused_computation.38.clone.1 | convolution fusion | flops 82903040 | bytes 7733248 | tf_op jit(solution)/shard_map/while/body/eval_jaxpr/niwpj,wpvq->nviqj/dot_general | solution.py:41
  161.5 5.2 copy.133
  188.3 6.3 %fusion.128 = bf16[44,64,4,64]{3,0,2,1:T(8,128)(2,1)S(1)} fusion(f32[64,64,44,4,1]{1,2,4,3,0:T(8,128)} %fusion.123, f32[64,64,44,4,1]{1,2,4,3,0:T(8,128)} %fusion.126, bf16[64,14,4,64,1]{3,2,0,1,4:T(4,128)(2,1)} %bitcast.261, bf16[44,4,44,4]{2,0,1,3:T(8,128)(2,1)S(1)} %get-tuple-element.315), kind=kOutput, calls=%fused_computation.38.clone.1 | convolution fusion | flops 82903040 | bytes 7733248 | tf_op jit(solution)/shard_map/while/body/eval_jaxpr/niwpj,wpvq->nviqj/dot_general | solution.py:41
  194.6 5.2 copy.133
  221.4 6.3 %fusion.128 = bf16[44,64,4,64]{3,0,2,1:T(8,128)(2,1)S(1)} fusion(f32[64,64,44,4,1]{1,2,4,3,0:T(8,128)} %fusion.123, f32[64,64,44,4,1]{1,2,4,3,0:T(8,128)} %fusion.126, bf16[64,14,4,64,1]{3,2,0,1,4:T(4,128)(2,1)} %bitcast.261, bf16[44,4,44,4]{2,0,1,3:T(8,128)(2,1)S(1)} %get-tuple-element.315), kind=kOutput, calls=%fused_computation.38.clone.1 | convolution fusion | flops 82903040 | bytes 7733248 | tf_op jit(solution)/shard_map/while/body/eval_jaxpr/niwpj,wpvq->nviqj/dot_general | solution.py:41
  254.5 6.3 %fusion.128 = bf16[44,64,4,64]{3,0,2,1:T(8,128)(2,1)S(1)} fusion(f32[64,64,44,4,1]{1,2,4,3,0:T(8,128)} %fusion.123, f32[64,64,44,4,1]{1,2,4,3,0:T(8,128)} %fusion.126, bf16[64,14,4,64,1]{3,2,0,1,4:T(4,128)(2,1)} %bitcast.261, bf16[44,4,44,4]{2,0,1,3:T(8,128)(2,1)S(1)} %get-tuple-element.315), kind=kOutput, calls=%fused_computation.38.clone.1 | convolution fusion | flops 82903040 | bytes 7733248 | tf_op jit(solution)/shard_map/while/body/eval_jaxpr/niwpj,wpvq->nviqj/dot_general | solution.py:41
  287.6 6.3 %fusion.128 = bf16[44,64,4,64]{3,0,2,1:T(8,128)(2,1)S(1)} fusion(f32[64,64,44,4,1]{1,2,4,3,0:T(8,128)} %fusion.123, f32[64,64,44,4,1]{1,2,4,3,0:T(8,128)} %fusion.126, bf16[64,14,4,64,1]{3,2,0,1,4:T(4,128)(2,1)} %bitcast.261, bf16[44,4,44,4]{2,0,1,3:T(8,128)(2,1)S(1)} %get-tuple-element.315), kind=kOutput, calls=%fused_computation.38.clone.1 | convolution fusion | flops 82903040 | bytes 7733248 | tf_op jit(solution)/shard_map/while/body/eval_jaxpr/niwpj,wpvq->nviqj/dot_general | solution.py:41
  320.7 6.3 %fusion.128 = bf16[44,64,4,64]{3,0,2,1:T(8,128)(2,1)S(1)} fusion(f32[64,64,44,4,1]{1,2,4,3,0:T(8,128)} %fusion.123, f32[64,64,44,4,1]{1,2,4,3,0:T(8,128)} %fusion.126, bf16[64,14,4,64,1]{3,2,0,1,4:T(4,128)(2,1)} %bitcast.261, bf16[44,4,44,4]{2,0,1,3:T(8,128)(2,1)S(1)} %get-tuple-element.315), kind=kOutput, calls=%fused_computation.38.clone.1 | convolution fusion | flops 82903040 | bytes 7733248 | tf_op jit(solution)/shard_map/while/body/eval_jaxpr/niwpj,wpvq->nviqj/dot_general | solution.py:41
  338.4 271.0 %while.20 = (s32[]{:T(128)}, f32[8,64,256]{2,1,0:T(8,128)}, bf16[2,10,64,256]{3,2,1,0:T(8,128)(2,1)S(1)}, s32[8]{0:T(128)S(1)}, bf16[8,64,2816]{2,1,0:T(8,128)(2...) while((s32[]{:T(128)}, f32[8,64,256]{2,1,0:T(8,128)}, ...), condition=%wide.region_1.2_spmd, body=%wide.region_0.1_spmd.sunk | while | flops 441188352 | bytes 42242408 | solution.py:84
  356.3 6.3 %fusion.110 = bf16[44,64,4,64]{3,0,2,1:T(8,128)(2,1)S(1)} fusion(f32[64,64,44,4,1]{1,2,4,3,0:T(8,128)} %fusion.105, f32[64,64,44,4,1]{1,2,4,3,0:T(8,128)} %fusion.108, bf16[64,14,4,64,1]{3,2,0,1,4:T(4,128)(2,1)} %bitcast.262, bf16[44,4,44,4]{2,0,1,3:T(8,128)(2,1)} %copy-done), kind=kOutput, calls=%fused_computation.3.clone.1 | convolution fusion | flops 82903040 | bytes 15007744 | tf_op jit(solution)/shard_map/while/body/eval_jaxpr/niwpj,wpvq->nviqj/dot_general | solution.py:41
  390.1 6.3 %fusion.110 = bf16[44,64,4,64]{3,0,2,1:T(8,128)(2,1)S(1)} fusion(f32[64,64,44,4,1]{1,2,4,3,0:T(8,128)} %fusion.105, f32[64,64,44,4,1]{1,2,4,3,0:T(8,128)} %fusion.108, bf16[64,14,4,64,1]{3,2,0,1,4:T(4,128)(2,1)} %bitcast.262, bf16[44,4,44,4]{2,0,1,3:T(8,128)(2,1)} %copy-done), kind=kOutput, calls=%fused_computation.3.clone.1 | convolution fusion | flops 82903040 | bytes 15007744 | tf_op jit(solution)/shard_map/while/body/eval_jaxpr/niwpj,wpvq->nviqj/dot_general | solution.py:41
  424.0 6.3 %fusion.110 = bf16[44,64,4,64]{3,0,2,1:T(8,128)(2,1)S(1)} fusion(f32[64,64,44,4,1]{1,2,4,3,0:T(8,128)} %fusion.105, f32[64,64,44,4,1]{1,2,4,3,0:T(8,128)} %fusion.108, bf16[64,14,4,64,1]{3,2,0,1,4:T(4,128)(2,1)} %bitcast.262, bf16[44,4,44,4]{2,0,1,3:T(8,128)(2,1)} %copy-done), kind=kOutput, calls=%fused_computation.3.clone.1 | convolution fusion | flops 82903040 | bytes 15007744 | tf_op jit(solution)/shard_map/while/body/eval_jaxpr/niwpj,wpvq->nviqj/dot_general | solution.py:41
  457.9 6.3 %fusion.110 = bf16[44,64,4,64]{3,0,2,1:T(8,128)(2,1)S(1)} fusion(f32[64,64,44,4,1]{1,2,4,3,0:T(8,128)} %fusion.105, f32[64,64,44,4,1]{1,2,4,3,0:T(8,128)} %fusion.108, bf16[64,14,4,64,1]{3,2,0,1,4:T(4,128)(2,1)} %bitcast.262, bf16[44,4,44,4]{2,0,1,3:T(8,128)(2,1)} %copy-done), kind=kOutput, calls=%fused_computation.3.clone.1 | convolution fusion | flops 82903040 | bytes 15007744 | tf_op jit(solution)/shard_map/while/body/eval_jaxpr/niwpj,wpvq->nviqj/dot_general | solution.py:41
  491.8 6.3 %fusion.110 = bf16[44,64,4,64]{3,0,2,1:T(8,128)(2,1)S(1)} fusion(f32[64,64,44,4,1]{1,2,4,3,0:T(8,128)} %fusion.105, f32[64,64,44,4,1]{1,2,4,3,0:T(8,128)} %fusion.108, bf16[64,14,4,64,1]{3,2,0,1,4:T(4,128)(2,1)} %bitcast.262, bf16[44,4,44,4]{2,0,1,3:T(8,128)(2,1)} %copy-done), kind=kOutput, calls=%fused_computation.3.clone.1 | convolution fusion | flops 82903040 | bytes 15007744 | tf_op jit(solution)/shard_map/while/body/eval_jaxpr/niwpj,wpvq->nviqj/dot_general | solution.py:41
  525.6 6.3 %fusion.110 = bf16[44,64,4,64]{3,0,2,1:T(8,128)(2,1)S(1)} fusion(f32[64,64,44,4,1]{1,2,4,3,0:T(8,128)} %fusion.105, f32[64,64,44,4,1]{1,2,4,3,0:T(8,128)} %fusion.108, bf16[64,14,4,64,1]{3,2,0,1,4:T(4,128)(2,1)} %bitcast.262, bf16[44,4,44,4]{2,0,1,3:T(8,128)(2,1)} %copy-done), kind=kOutput, calls=%fused_computation.3.clone.1 | convolution fusion | flops 82903040 | bytes 15007744 | tf_op jit(solution)/shard_map/while/body/eval_jaxpr/niwpj,wpvq->nviqj/dot_general | solution.py:41
  559.5 6.3 %fusion.110 = bf16[44,64,4,64]{3,0,2,1:T(8,128)(2,1)S(1)} fusion(f32[64,64,44,4,1]{1,2,4,3,0:T(8,128)} %fusion.105, f32[64,64,44,4,1]{1,2,4,3,0:T(8,128)} %fusion.108, bf16[64,14,4,64,1]{3,2,0,1,4:T(4,128)(2,1)} %bitcast.262, bf16[44,4,44,4]{2,0,1,3:T(8,128)(2,1)} %copy-done), kind=kOutput, calls=%fused_computation.3.clone.1 | convolution fusion | flops 82903040 | bytes 15007744 | tf_op jit(solution)/shard_map/while/body/eval_jaxpr/niwpj,wpvq->nviqj/dot_general | solution.py:41
  593.4 6.3 %fusion.110 = bf16[44,64,4,64]{3,0,2,1:T(8,128)(2,1)S(1)} fusion(f32[64,64,44,4,1]{1,2,4,3,0:T(8,128)} %fusion.105, f32[64,64,44,4,1]{1,2,4,3,0:T(8,128)} %fusion.108, bf16[64,14,4,64,1]{3,2,0,1,4:T(4,128)(2,1)} %bitcast.262, bf16[44,4,44,4]{2,0,1,3:T(8,128)(2,1)} %copy-done), kind=kOutput, calls=%fused_computation.3.clone.1 | convolution fusion | flops 82903040 | bytes 15007744 | tf_op jit(solution)/shard_map/while/body/eval_jaxpr/niwpj,wpvq->nviqj/dot_general | solution.py:41
  (455 shorter events, 380.1 us)
Async XLA Ops:
  6.5 30.3 %copy-start.6 = (bf16[8,64,256]{2,1,0:T(8,128)(2,1)S(1)}, bf16[8,64,256]{2,1,0:T(8,128)(2,1)}, u32[]{:S(2)}) copy-start(bf16[8,64,256]{2,1,0:T(8,128)(2,1)} %param.16) | copy-start | bytes 786436
  6.5 30.3 %copy-start.7 = (bf16[1,8,64,256]{3,2,1,0:T(8,128)(2,1)S(1)}, bf16[1,8,64,256]{3,2,1,0:T(8,128)(2,1)}, u32[]{:S(2)}) copy-start(bf16[1,8,64,256]{3,2,1,0:T(8,128)(2,1)} %param.15) | copy-start | bytes 786436
  6.5 28.1 %copy-start.11 = (s32[8]{0:T(128)S(1)}, s32[8]{0:T(128)}, u32[]{:S(2)}) copy-start(s32[8]{0:T(128)} %param.19) | copy-start | bytes 100
  6.5 30.2 %copy-start.8 = (bf16[44,4,44,4]{2,3,1,0:T(4,128)(2,1)S(1)}, bf16[44,4,44,4]{2,3,1,0:T(4,128)(2,1)}, u32[]{:S(2)}) copy-start(bf16[44,4,44,4]{2,3,1,0:T(4,128)(2,1)} %param.17) | copy-start | bytes 185860
  6.5 331.0 %all-gather.2.cloned.1.call-start = ((), (), s32[]{:S(2)}) async-start(), calls=%async_computation | async-start | bytes 3604480 | tf_op jit(solution)/shard_map/all_gather | solution.py:76
  6.6 19.4 %collective-permute-start.2 = (bf16[8,16,2816]{2,1,0:T(8,128)(2,1)}, bf16[8,16,2816]{2,1,0:T(8,128)(2,1)S(1)}, u32[]{:S(2)}, u32[]{:S(2)}) collective-permute-start(bf16[8,16,2816]{2,1,0:T(8,128)(2,1)} %param.13), channel_id=1, source_target_pairs={{0,8},{8,0},{16,24},{24,16},{1,9},{9,1},{17,25},{25,17},{2,10},{10... | collective-permute-start | bytes 2162696 | tf_op jit(solution)/shard_map/ppermute | solution.py:59
  27.6 40.7 %collective-permute-start.3 = (bf16[8,32,2816]{2,1,0:T(8,128)(2,1)S(1)}, bf16[8,32,2816]{2,1,0:T(8,128)(2,1)}, u32[]{:S(2)}, u32[]{:S(2)}) collective-permute-start(bf16[8,32,2816]{2,1,0:T(8,128)(2,1)S(1)} %maximum_select_fusion.1), channel_id=1, source_target_pairs={{0,16},{8,24},{16,0},{24,8},{1,17},{9,25},{17,1},{25,9},{2,18},{10... | collective-permute-start | bytes 4325384 | tf_op jit(solution)/shard_map/ppermute | solution.py:59
  30.3 6.5 %collective-permute-start.1 = (bf16[2,1,64,256]{3,2,1,0:T(8,128)(2,1)S(1)}, bf16[2,1,64,256]{3,2,1,0:T(8,128)(2,1)S(1)}, u32[]{:S(2)}, u32[]{:S(2)}) collective-permute-start(bf16[2,1,64,256]{3,2,1,0:T(8,128)(2,1)S(1)} %get-tuple-element.146), channel_id=1, source_target_pairs={{1,0},{2,1},{3,2},{4,3},{5,4},{6,5},{7,6},{9,8},{10,9},{11,10},{12... | collective-permute-start | bytes 196616 | tf_op jit(solution)/shard_map/ppermute | solution.py:16
  31.6 5.2 collective-permute-start
  72.7 5.8 copy-start.2
  105.8 5.8 copy-start.2
  138.9 5.8 copy-start.2
  172.0 5.8 copy-start.2
  205.1 5.8 copy-start.2
  238.2 5.8 copy-start.2
  271.3 5.8 copy-start.2
  304.4 5.8 copy-start.2
  338.4 271.0 %copy-start.9 = (pred[8,256]{1,0:T(8,128)(4,1)S(1)}, pred[8,256]{1,0:T(8,128)(4,1)}, u32[]{:S(2)}) copy-start(pred[8,256]{1,0:T(8,128)(4,1)} %broadcast_compare_fusion) | copy-start | bytes 6148
  338.4 271.0 %copy-start.10 = (pred[8,64]{1,0:T(8,128)(4,1)S(1)}, pred[8,64]{1,0:T(8,128)(4,1)}, u32[]{:S(2)}) copy-start(pred[8,64]{1,0:T(8,128)(4,1)} %iota_compare_fusion) | copy-start | bytes 1540
  372.2 5.8 copy-start.4
  406.1 5.8 copy-start.4
  440.0 5.8 copy-start.4
  473.8 5.8 copy-start.4
  507.7 5.8 copy-start.4
  (35 other events, 138.1 us)
Sparse Core Ops, SparseCore 0:
  34.7 49.9 all-gather.1
